TPU v7x, 512 devices: a whole 4x4x16 slice. The times are simulated.
512 devices in a mesh: section: 8 (over x, core), expert: 64 (over y, z).
Axes of the slice: x: 4, y: 4, z: 16, core: 2. Of those that a mesh axis runs over, the one named last changes fastest.
Arguments:
- tokens: bfloat16 [8192, 4096], P('expert', 'section'), may hold values from -6 to 6
- expert_ids: int32 [8192, 8], P('expert'), may hold values from 0 to 63, all different within a row; in each aligned block of 128 rows (0 to 127, 128 to 255, ...) at most 20 rows name the same one
- numerators: int32 [8192, 8], P('expert'), may hold values from 1 to 255
- gate_up_weight: bfloat16 [64, 4096, 3072], P('expert', None, 'section'), may hold values from -0.09375 to 0.09375
- down_weight: bfloat16 [64, 1536, 4096], P('expert', None, 'section'), may hold values from -0.15625 to 0.15625
Outputs:
- mixed: bfloat16 [8192, 4096], P('expert', 'section')
Inputs may be any that keep to these rules, and one draw needn't show every extreme that they name: `expert_ids`: each row names 8 different experts. Among the rows of one index of expert (aligned blocks of 128 rows) no expert is named more than 20 times, and in every draw some expert is named exactly 20 times there.
All inputs are finite; a program needn't handle non-finite values.
Results may differ from a plain program's by a relative error of at most 0.0057.
Values may be sent and summed in bfloat16 or wider, within the bound.
A program may use at most 128 MiB of HBM per device.

v0:
```python
import jax
import jax.numpy as jnp
from jax import lax
from jax.sharding import PartitionSpec as P

BLOCK_UNITS = 64


denominator = 256.0


def shards(tokens, expert_ids, numerators, gate_up_weight, down_weight):
    tok_rows = tokens.shape[0]
    top_count = expert_ids.shape[1]
    experts = lax.axis_size("expert") * gate_up_weight.shape[0]
    capacity = tok_rows * top_count * 5 // (4 * experts)
    flat = expert_ids.reshape(-1)
    hits = (flat[:, None] == jnp.arange(experts, dtype=jnp.int32)[None, :]).astype(jnp.int32)
    rank = jnp.sum((jnp.cumsum(hits, axis=0) - hits) * hits, axis=1)
    slot = flat * capacity + rank
    source = jnp.arange(tok_rows * top_count, dtype=jnp.int32) // top_count
    table = jnp.full((experts * capacity,), tok_rows, jnp.int32).at[slot].set(source)
    outgoing = jnp.take(tokens, table, axis=0, mode="fill", fill_value=0)
    slices = lax.all_to_all(outgoing, "expert", split_axis=0, concat_axis=0, tiled=True)
    arrived = lax.all_gather(slices, "section", axis=1, tiled=True)
    slot_rows = arrived.shape[0]
    local_units = gate_up_weight.shape[2] // 2
    both = jnp.dot(arrived, gate_up_weight[0], preferred_element_type=jnp.float32)
    split_up = both.reshape(slot_rows, local_units // BLOCK_UNITS, 2, BLOCK_UNITS)
    gate = split_up[:, :, 0, :].reshape(slot_rows, local_units)
    up = split_up[:, :, 1, :].reshape(slot_rows, local_units)
    hidden = (jax.nn.silu(gate) * up).astype(jnp.bfloat16)
    all_hidden = lax.all_gather(hidden, "section", axis=1, tiled=True)
    result = jnp.dot(all_hidden, down_weight[0], preferred_element_type=jnp.float32).astype(
        jnp.bfloat16
    )
    returned = lax.all_to_all(result, "expert", split_axis=0, concat_axis=0, tiled=True)
    picked = jnp.take(returned, slot, axis=0).astype(jnp.float32)
    weights = numerators.reshape(-1).astype(jnp.float32) / denominator
    weighted = (picked * weights[:, None]).reshape(tok_rows, top_count, -1)
    return jnp.sum(weighted, axis=1).astype(jnp.bfloat16)


def solution(mesh):
    in_specs = (
        P("expert", "section"),
        P("expert", None),
        P("expert", None),
        P("expert", None, "section"),
        P("expert", None, "section"),
    )
    out_specs = P("expert", "section")
    return jax.shard_map(shards, mesh=mesh, in_specs=in_specs, out_specs=out_specs, check_vma=False)
```

profile of v0, /device:TPU:24, one launch (start us, length us, event | category | flops | bytes accessed | tf_op | source)
XLA Modules:
  0.0 357.1 jit_solution(2606890356216971257)
XLA Ops:
  6.5 0.0 copy-start
  6.5 0.0 copy-start.1
  6.5 0.0 all-gather.3.cloned.1.call-start
  6.5 0.9 copy.16
  7.5 0.1 eq.26
  7.6 0.1 reshape.90
  7.6 0.7 broadcast_multiply_fusion
  8.4 18.0 %reduce-window.6 = s32[64,8,128]{2,1,0:T(8,128)S(1)} reduce-window(s32[64,8,128]{2,1,0:T(8,128)S(1)} %fusion.10, s32[]{:T(128)} %constant.52.clone.1), window={size=1x1x128 pad=0_0x0_0x127_0}, to_apply=%region_0.0 | reduce-window | flops 8323072 | bytes 524292 | tf_op jit(solution)/shard_map/reduce-window
  26.4 0.1 slice.20
  26.5 0.1 copy.18
  26.7 0.1 copy.19
  26.8 0.1 broadcast_add_fusion
  26.9 0.1 copy.22
  27.0 0.1 mul.41
  27.1 0.1 fusion.9
  27.2 4.3 %scatter_custom_fusion = s32[1280]{0:T(1024)S(1)} fusion(s32[1024]{0:T(1024)S(1)} %bitcast.60, s32[1024]{0:T(1024)S(1)} %add_select_fusion, s32[]{:T(128)} %constant.55.clone.1), kind=kCustom, calls=%fused_computation.37 | custom fusion | bytes 5124 | tf_op jit(solution)/shard_map/scatter | solution.py:22
  31.6 0.0 copy-done.1
  31.6 4.7 %gather_fusion = bf16[1280,512]{1,0:T(8,128)(2,1)} fusion(bf16[128,512]{1,0:T(8,128)(2,1)S(1)} %copy-done.1, s32[2048]{0:T(1024)S(1)} %pad_clamp_fusion), kind=kCustom, calls=%fused_computation | custom fusion | bytes 2626560 | tf_op jit(solution)/shard_map/jit(_take)/gather | solution.py:23
  36.3 2.2 gather.13
  38.5 0.1 broadcast_in_dim.32
  38.7 0.3 broadcast_select_fusion
  38.9 94.7 %all_to_all.21 = bf16[64,20,512]{2,1,0:T(8,128)(2,1)S(1)} all-to-all(bf16[64,20,512]{2,1,0:T(8,128)(2,1)S(1)} %broadcast_select_fusion), channel_id=1, replica_groups=mesh['section'=8,'expert'=64] {'expert'}, dimensions={0} | all-to-all | bytes 2621440 | tf_op jit(solution)/shard_map/all_to_all | solution.py:24
  133.6 1.2 all_to_all.15
  134.8 0.0 all-gather.3.cloned.1.call-update
  134.8 0.0 all-gather.5.cloned.1.call-start
  134.9 4.7 %copy.23 = bf16[1,4096,384]{1,2,0:T(8,128)(2,1)} copy(bf16[1,4096,384]{2,1,0:T(8,128)(2,1)} %param.8) | data formatting | bytes 6291456 | tf_op args[3]
  139.6 54.0 %all-gather.3.cloned.1.call-done = bf16[1280,4096]{1,0:T(8,128)(2,1)} async-done(((bf16[1280,512]{1,0:T(8,128)(2,1)}), bf16[1280,4096]{1,0:T(8,128)(2,1)}) %all-gather.3.cloned.1.call-update) | async-done | bytes 10485776 | tf_op jit(solution)/shard_map/all_gather | solution.py:25
  193.6 8.8 %fusion = f32[1280,3,2,64]{0,3,2,1:T(8,128)S(1)} fusion(bf16[3,2,64,4096]{3,2,1,0:T(8,128)(2,1)} %bitcast.56, bf16[1280,4096]{1,0:T(8,128)(2,1)} %all-gather.3.cloned.1.call-done), kind=kOutput, calls=%fused_computation.3 | convolution fusion | flops 4026531840 | bytes 15597568 | tf_op jit(solution)/shard_map/dot_general | solution.py:28
  202.3 0.1 fusion.16
  202.5 1.1 fusion.3
  203.5 0.0 all-gather.5.cloned.1.call-update
  203.6 39.2 %all-gather.5.cloned.1.call-done = bf16[1280,1536]{0,1:T(8,128)(2,1)} async-done(((bf16[1280,192]{0,1:T(8,128)(2,1)}), bf16[1280,1536]{0,1:T(8,128)(2,1)}) %all-gather.5.cloned.1.call-update) | async-done | bytes 3932176 | tf_op jit(solution)/shard_map/all_gather | solution.py:33
  242.8 0.0 copy-done
  242.8 4.3 %convolution_convert_fusion = bf16[1280,512]{1,0:T(8,128)(2,1)S(1)} fusion(bf16[1280,1536]{0,1:T(8,128)(2,1)} %all-gather.5.cloned.1.call-done, bf16[1,1536,512]{2,1,0:T(8,128)(2,1)S(1)} %copy-done), kind=kOutput, calls=%fused_computation.5 | convolution fusion | flops 2013921280 | bytes 6815744 | tf_op jit(solution)/shard_map/dot_general | solution.py:34
  247.1 1.3 all_to_all.16
  248.4 0.0 copy-start.2
  248.4 0.0 copy-start.3
  248.4 16.2 %all-to-all-start.1 = ((bf16[64,20,512]{2,1,0:T(8,128)(2,1)}), bf16[64,20,512]{2,1,0:T(8,128)(2,1)}, u32[]{:S(2)}, u32[]{:S(2)}) async-start(bf16[64,20,512]{2,1,0:T(8,128)(2,1)} %all_to_all.16), calls=%async_computation.1 | async-start | bytes 3145728 | tf_op jit(solution)/shard_map/all_to_all | solution.py:37
  264.6 0.1 reduce_sum.23
  264.8 0.0 copy-done.2
  264.8 0.1 copy.21
  264.9 0.0 copy-done.3
  265.0 0.1 copy.24
  265.1 75.1 %all-to-all-done.1 = bf16[64,20,512]{2,1,0:T(8,128)(2,1)} async-done(((bf16[64,20,512]{2,1,0:T(8,128)(2,1)}), bf16[64,20,512]{2,1,0:T(8,128)(2,1)}, u32[]{:S(2)}, u32[]{:S(2)}) %all-to-all-start.1) | async-done | bytes 1310752 | tf_op jit(solution)/shard_map/all_to_all | solution.py:37
  340.2 2.3 all_to_all.18
  342.5 5.1 %gather_fusion.1 = bf16[1024,512]{1,0:T(8,128)(2,1)} fusion(bf16[1280,512]{1,0:T(8,128)(2,1)S(1)} %all_to_all.18, s32[1024]{0:T(1024)S(1)} %broadcast_clamp_fusion), kind=kCustom, calls=%fused_computation.1 | custom fusion | bytes 2101248 | tf_op jit(solution)/shard_map/jit(_take)/gather | solution.py:38
  347.5 2.7 multiply_reduce_fusion
  (12 shorter events, 0.2 us)
Async XLA Ops:
  6.5 236.3 %copy-start = (bf16[1,1536,512]{2,1,0:T(8,128)(2,1)S(1)}, bf16[1,1536,512]{2,1,0:T(8,128)(2,1)}, u32[]{:S(2)}) copy-start(bf16[1,1536,512]{2,1,0:T(8,128)(2,1)} %param.9) | copy-start | bytes 4718596
  6.5 25.0 %copy-start.1 = (bf16[128,512]{1,0:T(8,128)(2,1)S(1)}, bf16[128,512]{1,0:T(8,128)(2,1)}, u32[]{:S(2)}) copy-start(bf16[128,512]{1,0:T(8,128)(2,1)} %param.5) | copy-start | bytes 393220
  6.5 187.0 %all-gather.3.cloned.1.call-start = ((), (), s32[]{:S(2)}) async-start(), calls=%async_computation.2 | async-start | bytes 11796480 | tf_op jit(solution)/shard_map/all_gather | solution.py:25
  134.8 108.0 %all-gather.5.cloned.1.call-start = ((), (), s32[]{:S(2)}) async-start(), calls=%async_computation.3 | async-start | bytes 4423680 | tf_op jit(solution)/shard_map/all_gather | solution.py:33
  248.4 16.3 %copy-start.2 = (s32[128,8]{0,1:T(8,128)S(1)}, s32[128,8]{0,1:T(8,128)}, u32[]{:S(2)}) copy-start(s32[128,8]{0,1:T(8,128)} %param.6) | copy-start | bytes 12292
  248.4 16.5 %copy-start.3 = (s32[128,8]{0,1:T(8,128)S(1)}, s32[128,8]{0,1:T(8,128)}, u32[]{:S(2)}) copy-start(s32[128,8]{0,1:T(8,128)} %param.7) | copy-start | bytes 12292
  248.4 91.7 %all-to-all-start.1 = ((bf16[64,20,512]{2,1,0:T(8,128)(2,1)}), bf16[64,20,512]{2,1,0:T(8,128)(2,1)}, u32[]{:S(2)}, u32[]{:S(2)}) async-start(bf16[64,20,512]{2,1,0:T(8,128)(2,1)} %all_to_all.16), calls=%async_computation.1 | async-start | bytes 3145728 | tf_op jit(solution)/shard_map/all_to_all | solution.py:37
Sparse Core Ops, SparseCore 0:
  134.9 58.5 all-gather.2
  203.7 39.0 all-gather.4
where the time goes:
time: 358 us; the launch traced here: 357 us
  waiting for transfers between devices  168 us (47%)
  blocking collectives  94.7 us (26%)
  local copies, waits for them, and re-layouts  28.1 us (8%)
  other arithmetic  23 us (6%)
  starting transfers between devices  16.2 us (5%)
  between operations  13.6 us (4%)
  matrix products  13.1 us (4%)
    all_to_all x1, blocking collectives, shards(): lax.all_to_all(outgoing, 'expert', split_axis=0, concat_axis=0, tiled=True)  94.7 us
    all_to_all x1, waiting for transfers between devices, shards(): lax.all_to_all(result, 'expert', split_axis=0, concat_axis=0, tiled=True)  75.1 us
    all_gather x1, waiting for transfers between devices, shards(): arrived = lax.all_gather(slices, 'section', axis=1, tiled=True)  54 us
    all_gather x1, waiting for transfers between devices, shards(): all_hidden = lax.all_gather(hidden, 'section', axis=1, tiled=True)  39.2 us
    another operation x3, other arithmetic  18.2 us
    all_to_all x1, starting transfers between devices, shards(): lax.all_to_all(result, 'expert', split_axis=0, concat_axis=0, tiled=True)  16.2 us
    dot_general x1, matrix products, shards(): jnp.dot(arrived, gate_up_weight[0], preferred_element_type=jnp.float32)  8.76 us
  transfers between devices with their start and end apart: 3, of which 3 were waited for; matrix products, arithmetic and copies ran while one was open for 1% of the time, Pallas kernels for 0%

commit v1 on v0

v1 whole, which is shorter than its diff:
```python
import functools

import jax
import jax.numpy as jnp
from jax import lax
from jax.experimental import pallas as pl
from jax.experimental.pallas import tpu as pltpu
from jax.sharding import PartitionSpec as P

MESH = pl.DeviceIdType.MESH
BF = jnp.bfloat16
F32 = jnp.float32

NX, NY, NZ = 4, 4, 16
CAP = 20
GROUPS = ((6, -7, 7, -8), (4, -5, 5, -6), (2, -3, 3, -4), (0, -1, 1, -2))
PLACE = {off: (g, i) for g, offs in enumerate(GROUPS) for i, off in enumerate(offs)}
ORDER = (
    "A1", "A2", "S3", "A3", "Y3", "A4", "S2", "A5", "Y2", "A6", "S1", "X3",
    "A7", "Y1", "A8", "S0", "Z3", "Y0", "M3", "X2", "H3", "Z2", "I3", "M2",
    "J3", "H2", "N3", "X0", "I2", "Z0", "J2", "M0", "N2", "H0", "C3", "C2",
    "X1", "I0", "Z1", "J0", "M1", "N0", "H1", "C0", "R0", "R1", "I1", "J1",
    "N1", "C1", "R2", "R3", "R4", "R5", "R6", "R7",
)


def kernel(
    tok_in, route_in, wgu_hbm, wd_hbm, out_ref,
    tok, route, wgu, wd, wsel, ysend, xfull, acc1, hx_send, hx_recv, hfull, acc2, ret, back, part,
    dsend, usend, drecv, urecv,
    wg_sem, wd_sem, tok_s, tok_r, rt_s, rt_r, y_s, y_r, x_s, x_r, xc_s, xc_r,
    hx_s, hx_r, h_s, h_r, hc_s, hc_r, b_s, b_r, d_s, d_r, u_s, u_r,
):
    sec, exp = lax.axis_index("section"), lax.axis_index("expert")
    x, core = sec // 2, sec % 2
    y, z = exp // NZ, exp % NZ
    z_up = (sec, y * NZ + (z + 1) % NZ)
    z_dn = (sec, y * NZ + (z + NZ - 1) % NZ)
    y_at = [(sec, ((y + o) % NY) * NZ + z) for o in range(NY)]
    x_up = (((x + 1) % NX) * 2 + core, exp)
    x_dn = (((x + NX - 1) % NX) * 2 + core, exp)
    sib = (x * 2 + (1 - core), exp)
    peers = [z_up, z_dn, y_at[1], y_at[2], y_at[3], x_up, x_dn, sib]

    rows = NY * 4 * CAP
    quarter = 4 * CAP
    half = rows // 2
    feat = tok_in.shape[1]
    nsec = 2 * NX
    pend = []

    def remote(src, dst, ss, rs, dev):
        c = pltpu.make_async_remote_copy(
            src_ref=src, dst_ref=dst, send_sem=ss, recv_sem=rs, device_id=dev, device_id_type=MESH
        )
        c.start()
        pend.append(c)
        return c

    def landed(dst, rs):
        pltpu.make_async_remote_copy(
            src_ref=dst, dst_ref=dst, send_sem=rs, recv_sem=rs, device_id=sib, device_id_type=MESH
        ).wait_recv()

    for o in range(NX):
        for c in range(2):
            s = ((x + o) % NX) * 2 + (core + c) % 2
            pltpu.make_async_copy(
                wgu_hbm.at[0, pl.ds(pl.multiple_of(s * feat, feat), feat), :],
                wgu.at[o * 2 + c], wg_sem,
            ).start()
    units = wd_hbm.shape[1] // NX
    third = units // 6
    for o in range(NX):
        base = ((x + o) % NX) * units
        for frm, to, size in ((0, 0, 3), (5, 3, 1), (3, 4, 2)):
            pltpu.make_async_copy(
                wd_hbm.at[0, pl.ds(pl.multiple_of(base + frm * third, third), size * third), :],
                wd.at[o, pl.ds(to * third, size * third), :], wd_sem,
            ).start()

    barrier = pltpu.get_barrier_semaphore()
    for p in peers:
        pl.semaphore_signal(barrier, inc=1, device_id=p, device_id_type=MESH)
    pl.semaphore_wait(barrier, len(peers))

    def tslot(off):
        g, i = PLACE[off]
        return tok.at[g, pl.ds(i * 128, 128), :], route.at[g, i]

    def send_block(src, rsrc, off_there, dev):
        td, rd = tslot(off_there)
        k = off_there + 8
        remote(rsrc, rd, rt_s.at[k], rt_r.at[k], dev)
        remote(src, td, tok_s.at[k], tok_r.at[k], dev)

    send_block(tok_in, route_in, -1, z_up)
    send_block(tok_in, route_in, 1, z_dn)
    own_t, own_r = tslot(0)
    own_t[...] = tok_in[...]
    own_r[...] = route_in[...]

    tri = (
        lax.broadcasted_iota(jnp.int32, (128, 128), 0) < lax.broadcasted_iota(jnp.int32, (128, 128), 1)
    ).astype(F32).astype(BF)
    slot_iota = lax.broadcasted_iota(jnp.int32, (quarter, 128), 0).astype(F32)

    def gather_step(j):
        for off, dev, more in ((-j, z_up, j < 8), (j, z_dn, j < 7)):
            if off == 8:
                continue
            t, r = tslot(off)
            landed(r, rt_r.at[off + 8])
            landed(t, tok_r.at[off + 8])
            if more:
                send_block(t, r, off - 1 if off < 0 else off + 1, dev)

    def select(g):
        hits, weights = [], []
        for b in range(4):
            info = route[g, b].astype(F32)
            ids, nums = info[:8], info[8:]
            for o in range(NY):
                e = (((y + o) % NY) * NZ + z).astype(F32)
                hit = jnp.where(ids == e, 1.0, 0.0)
                hits.append(jnp.sum(hit, axis=0, keepdims=True))
                weights.append(jnp.sum(hit * nums, axis=0, keepdims=True) * (1.0 / 256.0))
        hit_all = jnp.concatenate(hits, axis=0)
        rank = jnp.dot(hit_all.astype(BF), tri, preferred_element_type=F32)
        code = jnp.where(hit_all > 0.5, rank, -1000.0)
        sel_cols = []
        for b in range(4):
            col, wcol = [], []
            for o in range(NY):
                r = b * NY + o
                same = slot_iota == code[r:r + 1] + float(b * CAP)
                col.append(jnp.where(same, 1.0, 0.0))
                wcol.append(jnp.where(same, weights[r], 0.0))
            wsel[g, :, b * 128:(b + 1) * 128] = jnp.concatenate(wcol, axis=0).astype(BF)
            sel_cols.append(jnp.concatenate(col, axis=0).astype(BF))
        sel = jnp.concatenate(sel_cols, axis=1)
        picked = jnp.dot(sel, tok[g], preferred_element_type=F32).astype(BF)
        for o in range(1, NY):
            ysend[g, pl.ds(o * quarter, quarter), :] = picked[o * quarter:(o + 1) * quarter]
            to = (NY - o) % NY
            remote(
                ysend.at[g, pl.ds(o * quarter, quarter), :],
                xfull.at[g, 0, pl.ds(to * quarter, quarter), :],
                y_s.at[g, to], y_r.at[g, to], y_at[o],
            )
        xfull[g, 0, pl.ds(0, quarter), :] = picked[:quarter]

    def rows_out(g):
        for o in range(1, NY):
            landed(xfull.at[g, 0, pl.ds(o * quarter, quarter), :], y_r.at[g, o])
        own = xfull.at[g, 0]
        remote(own, xfull.at[g, 6], x_s.at[g, 0], x_r.at[g, 0], x_up)
        remote(own, xfull.at[g, 2], x_s.at[g, 1], x_r.at[g, 1], x_dn)
        remote(own, xfull.at[g, 1], xc_s.at[g, 0], xc_r.at[g, 0], sib)

    def rows_forward(g):
        lo, hi = pl.ds(0, half), pl.ds(half, half)
        landed(xfull.at[g, 6], x_r.at[g, 0])
        remote(xfull.at[g, 6, lo, :], xfull.at[g, 4, lo, :], x_s.at[g, 2], x_r.at[g, 2], x_up)
        remote(xfull.at[g, 6], xfull.at[g, 7], xc_s.at[g, 1], xc_r.at[g, 1], sib)
        landed(xfull.at[g, 2], x_r.at[g, 1])
        remote(xfull.at[g, 2, hi, :], xfull.at[g, 4, hi, :], x_s.at[g, 3], x_r.at[g, 3], x_dn)
        remote(xfull.at[g, 2], xfull.at[g, 3], xc_s.at[g, 2], xc_r.at[g, 2], sib)

    def rows_last(g):
        lo, hi = pl.ds(0, half), pl.ds(half, half)
        landed(xfull.at[g, 4, lo, :], x_r.at[g, 2])
        landed(xfull.at[g, 4, hi, :], x_r.at[g, 3])
        remote(xfull.at[g, 4], xfull.at[g, 5], xc_s.at[g, 3], xc_r.at[g, 3], sib)

    state = {"w1": False, "w2": False}

    def first_matmul(g):
        if not state["w1"]:
            pltpu.make_async_copy(wgu, wgu, wg_sem).wait()
            state["w1"] = True
        for i, s in enumerate((1, 7, 3, 5)):
            landed(xfull.at[g, s], xc_r.at[g, i])
        acc1[...] = jnp.dot(xfull[g, 0], wgu[0], preferred_element_type=F32)

        def body(s, carry):
            acc1[...] += jnp.dot(xfull[g, s], wgu[s], preferred_element_type=F32)
            return carry

        lax.fori_loop(1, nsec, body, 0)
        lane = lax.broadcasted_iota(jnp.int32, (rows, 128), 1)
        parts = []
        for b in range(3):
            v = acc1[:, b * 128:(b + 1) * 128]
            other = pltpu.roll(v, 64, 1)
            low = lane < 64
            gate = jnp.where(low, v, other)
            up = jnp.where(low, other, v)
            parts.append(gate / (1.0 + jnp.exp(-gate)) * up)
        hx_send[g, :, 0:128] = jnp.where(lane < 64, parts[0], parts[1]).astype(BF)
        hx_send[g, :, 128:256] = parts[2].astype(BF)
        remote(
            hx_send.at[g, pl.ds(pl.multiple_of((1 - core) * half, half), half), :],
            hx_recv.at[g], hx_s.at[g], hx_r.at[g], sib,
        )

    mine = pl.ds(pl.multiple_of(core * half, half), half)
    mine_lo = pl.ds(pl.multiple_of(core * half, half // 2), half // 2)
    mine_hi = pl.ds(pl.multiple_of(core * half + half // 2, half // 2), half // 2)
    theirs = pl.ds(pl.multiple_of((1 - core) * half, half), half)

    def hidden_out(g):
        landed(hx_recv.at[g], hx_r.at[g])
        a = hx_send[g, mine, :].astype(F32)
        b = hx_recv[g].astype(F32)
        zero = core == 0
        first = jnp.where(zero, a, b)
        second = jnp.where(zero, b, a)
        lane = lax.broadcasted_iota(jnp.int32, (half, 128), 1)
        hfull[g, 0, mine, 0:128] = first[:, :128].astype(BF)
        hfull[g, 0, mine, 128:256] = jnp.where(lane < 64, first[:, 128:], second[:, 128:]).astype(BF)
        hfull[g, 0, mine, 256:384] = second[:, :128].astype(BF)
        own = hfull.at[g, 0, mine, :]
        remote(own, hfull.at[g, 3, mine, :], h_s.at[g, 0], h_r.at[g, 0], x_up)
        remote(own, hfull.at[g, 1, mine, :], h_s.at[g, 1], h_r.at[g, 1], x_dn)
        remote(own, hfull.at[g, 0, mine, :], hc_s.at[g, 0], hc_r.at[g, 0], sib)

    def hidden_forward(g):
        landed(hfull.at[g, 3, mine, :], h_r.at[g, 0])
        remote(hfull.at[g, 3, mine_lo, :], hfull.at[g, 2, mine_lo, :], h_s.at[g, 2], h_r.at[g, 2], x_up)
        remote(hfull.at[g, 3, mine, :], hfull.at[g, 3, mine, :], hc_s.at[g, 3], hc_r.at[g, 3], sib)
        landed(hfull.at[g, 1, mine, :], h_r.at[g, 1])
        remote(hfull.at[g, 1, mine_hi, :], hfull.at[g, 2, mine_hi, :], h_s.at[g, 3], h_r.at[g, 3], x_dn)
        remote(hfull.at[g, 1, mine, :], hfull.at[g, 1, mine, :], hc_s.at[g, 1], hc_r.at[g, 1], sib)

    def hidden_last(g):
        landed(hfull.at[g, 2, mine_lo, :], h_r.at[g, 2])
        landed(hfull.at[g, 2, mine_hi, :], h_r.at[g, 3])
        remote(hfull.at[g, 2, mine, :], hfull.at[g, 2, mine, :], hc_s.at[g, 2], hc_r.at[g, 2], sib)

    def second_matmul(g):
        if not state["w2"]:
            pltpu.make_async_copy(wd, wd, wd_sem).wait()
            state["w2"] = True
        for o in range(NX):
            landed(hfull.at[g, o, theirs, :], hc_r.at[g, o])
        acc2[...] = jnp.dot(hfull[g, 0], wd[0], preferred_element_type=F32)

        def body(o, carry):
            acc2[...] += jnp.dot(hfull[g, o], wd[o], preferred_element_type=F32)
            return carry

        lax.fori_loop(1, NX, body, 0)
        for o in range(1, NY):
            ret[g, pl.ds(o * quarter, quarter), :] = acc2[pl.ds(o * quarter, quarter), :].astype(BF)
            to = (NY - o) % NY
            remote(
                ret.at[g, pl.ds(o * quarter, quarter), :],
                back.at[g, pl.ds(to * quarter, quarter), :],
                b_s.at[g, to], b_r.at[g, to], y_at[o],
            )
        back[g, pl.ds(0, quarter), :] = acc2[pl.ds(0, quarter), :].astype(BF)

    def combine(g):
        for o in range(1, NY):
            landed(back.at[g, pl.ds(o * quarter, quarter), :], b_r.at[g, o])
        part[g] = lax.dot_general(
            wsel[g], back[g], (((0,), (0,)), ((), ())), preferred_element_type=F32
        )

    def share(off):
        g, i = PLACE[off]
        return part[g, pl.ds(i * 128, 128), :]

    def reduce_step(j):
        v = share(j - 8)
        if j > 0:
            landed(drecv.at[j - 1], d_r.at[j - 1])
            v = v + drecv[j - 1].astype(F32)
        dsend[j] = v.astype(BF)
        remote(dsend.at[j], drecv.at[j], d_s.at[j], d_r.at[j], z_dn)
        if j > 0:
            landed(urecv.at[j - 1], u_r.at[j - 1])
        if j < 7:
            v = share(7 - j)
            if j > 0:
                v = v + urecv[j - 1].astype(F32)
            usend[j] = v.astype(BF)
            remote(usend.at[j], urecv.at[j], u_s.at[j], u_r.at[j], z_up)

    steps = {
        "A": gather_step, "S": select, "Y": rows_out, "X": rows_forward, "Z": rows_last, "M": first_matmul,
        "H": hidden_out, "I": hidden_forward, "J": hidden_last, "N": second_matmul, "C": combine, "R": reduce_step,
    }
    for name in ORDER:
        steps[name[0]](int(name[1:]))

    landed(drecv.at[7], d_r.at[7])
    out_ref[...] = (share(0) + urecv[6].astype(F32) + drecv[7].astype(F32)).astype(BF)
    for c in pend:
        c.wait_send()


def shards(tokens, expert_ids, numerators, gate_up_weight, down_weight):
    route = jnp.concatenate([expert_ids.T, numerators.T], axis=0).astype(BF)
    feat = tokens.shape[1]
    rows = NY * 4 * CAP
    cols = gate_up_weight.shape[2]
    units = down_weight.shape[1] // NX
    dma = pltpu.SemaphoreType.DMA
    return pl.pallas_call(
        kernel,
        out_shape=jax.ShapeDtypeStruct(tokens.shape, BF),
        in_specs=[
            pl.BlockSpec(memory_space=pltpu.VMEM),
            pl.BlockSpec(memory_space=pltpu.VMEM),
            pl.BlockSpec(memory_space=pl.ANY),
            pl.BlockSpec(memory_space=pl.ANY),
        ],
        out_specs=pl.BlockSpec(memory_space=pltpu.VMEM),
        scratch_shapes=[
            pltpu.VMEM((4, 512, feat), BF),
            pltpu.VMEM((4, 4, 16, 128), BF),
            pltpu.VMEM((8, feat, cols), BF),
            pltpu.VMEM((NX, units, feat), BF),
            pltpu.VMEM((4, rows, 512), BF),
            pltpu.VMEM((4, rows, feat), BF),
            pltpu.VMEM((4, 8, rows, feat), BF),
            pltpu.VMEM((rows, cols), F32),
            pltpu.VMEM((4, rows, 256), BF),
            pltpu.VMEM((4, rows // 2, 256), BF),
            pltpu.VMEM((4, NX, rows, units), BF),
            pltpu.VMEM((rows, feat), F32),
            pltpu.VMEM((4, rows, feat), BF),
            pltpu.VMEM((4, rows, feat), BF),
            pltpu.VMEM((4, 512, feat), F32),
            pltpu.VMEM((8, 128, feat), BF),
            pltpu.VMEM((7, 128, feat), BF),
            pltpu.VMEM((8, 128, feat), BF),
            pltpu.VMEM((7, 128, feat), BF),
            dma, dma,
            dma((16,)), dma((16,)), dma((16,)), dma((16,)),
            dma((4, 4)), dma((4, 4)),
            dma((4, 4)), dma((4, 4)), dma((4, 4)), dma((4, 4)),
            dma((4,)), dma((4,)), dma((4, 4)), dma((4, 4)), dma((4, 4)), dma((4, 4)),
            dma((4, 4)), dma((4, 4)),
            dma((8,)), dma((8,)), dma((7,)), dma((7,)),
        ],
        compiler_params=pltpu.CompilerParams(
            collective_id=0, has_side_effects=True, vmem_limit_bytes=56 * 1024 * 1024
        ),
    )(tokens, route, gate_up_weight, down_weight)


def solution(mesh):
    in_specs = (
        P("expert", "section"),
        P("expert", None),
        P("expert", None),
        P("expert", None, "section"),
        P("expert", None, "section"),
    )
    out_specs = P("expert", "section")
    return jax.shard_map(shards, mesh=mesh, in_specs=in_specs, out_specs=out_specs, check_vma=False)
```

time: 358 us -> 166 us (0.46)
  the two profiles are of different devices: /device:TPU:24 before, /device:TPU:66 now
where the time goes in v1:
time: 166 us
  Pallas kernels  163 us (98%)
    pallas_call x1, Pallas kernels, shards(): pl.pallas_call(kernel, out_shape=jax.ShapeDtypeStruct(tokens.shape, BF),...  163 us

profile of v1, /device:TPU:66, one launch (start us, length us, event | category | flops | bytes accessed | tf_op | source)
XLA Modules:
  0.0 165.6 jit_solution(17346531082278539496)
XLA Ops:
  0.0 0.7 convert_bitcast_fusion
  0.7 0.6 pad_maximum_fusion.route_in
  1.3 162.7 %shard_map.55 = bf16[128,512]{1,0:T(8,128)(2,1)} custom-call(bf16[128,512]{1,0:T(8,128)(2,1)} %tok_in.1, bf16[16,128]{1,0:T(8,128)(2,1)} %pad_maximum_fusion.route_in, bf16[1,4096,384]{2,1,0:T(8,128)(2,1)} %wgu_hbm.1, bf16[1,1536,512]{2,1,0:T(8,128)(2,1)} %wd_hbm.1), custom_call_target="tpu_custom_call" | custom-call | tf_op jit(solution)/shard_map/pallas_call | solution.py:311
  164.0 1.6 copy.7

commit v2 on v1

--- a/solution.py
+++ b/solution.py
@@ -13,14 +13,18 @@
 
 NX, NY, NZ = 4, 4, 16
 CAP = 20
+AP, RP = 2, 4
 GROUPS = ((6, -7, 7, -8), (4, -5, 5, -6), (2, -3, 3, -4), (0, -1, 1, -2))
 PLACE = {off: (g, i) for g, offs in enumerate(GROUPS) for i, off in enumerate(offs)}
 ORDER = (
-    "A1", "A2", "S3", "A3", "Y3", "A4", "S2", "A5", "Y2", "A6", "S1", "X3",
-    "A7", "Y1", "A8", "S0", "Z3", "Y0", "M3", "X2", "H3", "Z2", "I3", "M2",
-    "J3", "H2", "N3", "X0", "I2", "Z0", "J2", "M0", "N2", "H0", "C3", "C2",
-    "X1", "I0", "Z1", "J0", "M1", "N0", "H1", "C0", "R0", "R1", "I1", "J1",
-    "N1", "C1", "R2", "R3", "R4", "R5", "R6", "R7",
+    "A1.0", "A1.1", "A2.0", "A2.1", "S3", "A3.0", "A3.1", "A4.0", "Y3", "A4.1", "S2", "A5.1",
+    "Y2", "A5.0", "A6.1", "A7.1", "X3", "A6.0", "S1", "X2", "A8.1", "A7.0", "Y1", "Z3",
+    "A8.0", "S0", "Z2", "M2", "Y0", "M3", "X0", "X1", "H2", "Z0", "M0", "H0",
+    "H3", "Z1", "M1", "I0", "H1", "J0", "I3", "N0", "I1", "I2", "J3", "C0",
+    "R0.1", "R0.3", "J1", "R0.2", "R0.0", "J2", "N1", "R1.1", "R1.2", "R1.0", "R1.3", "N2",
+    "C1", "R2.1", "R2.0", "R2.3", "R2.2", "N3", "R3.1", "R3.0", "C2", "R3.3", "R3.2", "R4.1",
+    "R4.0", "R4.3", "R4.2", "C3", "R5.1", "R5.0", "R5.3", "R5.2", "R6.1", "R6.0", "R6.3", "R6.2",
+    "R7.1", "R7.0", "R7.3", "R7.2",
 )
 
 
@@ -88,14 +92,17 @@
         g, i = PLACE[off]
         return tok.at[g, pl.ds(i * 128, 128), :], route.at[g, i]
 
-    def send_block(src, rsrc, off_there, dev):
+    def send_block(src, rsrc, off_there, dev, p):
         td, rd = tslot(off_there)
         k = off_there + 8
-        remote(rsrc, rd, rt_s.at[k], rt_r.at[k], dev)
-        remote(src, td, tok_s.at[k], tok_r.at[k], dev)
-
-    send_block(tok_in, route_in, -1, z_up)
-    send_block(tok_in, route_in, 1, z_dn)
+        cut = pl.ds(p * (128 // AP), 128 // AP)
+        if p == 0:
+            remote(rsrc, rd, rt_s.at[k], rt_r.at[k], dev)
+        remote(src.at[cut, :], td.at[cut, :], tok_s.at[k, p], tok_r.at[k, p], dev)
+
+    for p in range(AP):
+        send_block(tok_in, route_in, -1, z_up, p)
+        send_block(tok_in, route_in, 1, z_dn, p)
     own_t, own_r = tslot(0)
     own_t[...] = tok_in[...]
     own_r[...] = route_in[...]
@@ -105,15 +112,17 @@
     ).astype(F32).astype(BF)
     slot_iota = lax.broadcasted_iota(jnp.int32, (quarter, 128), 0).astype(F32)
 
-    def gather_step(j):
+    def gather_step(j, p):
+        cut = pl.ds(p * (128 // AP), 128 // AP)
         for off, dev, more in ((-j, z_up, j < 8), (j, z_dn, j < 7)):
             if off == 8:
                 continue
             t, r = tslot(off)
-            landed(r, rt_r.at[off + 8])
-            landed(t, tok_r.at[off + 8])
+            if p == 0:
+                landed(r, rt_r.at[off + 8])
+            landed(t.at[cut, :], tok_r.at[off + 8, p])
             if more:
-                send_block(t, r, off - 1 if off < 0 else off + 1, dev)
+                send_block(t, r, off - 1 if off < 0 else off + 1, dev, p)
 
     def select(g):
         hits, weights = [], []
@@ -268,35 +277,42 @@
             wsel[g], back[g], (((0,), (0,)), ((), ())), preferred_element_type=F32
         )
 
-    def share(off):
+    def share(off, p):
         g, i = PLACE[off]
-        return part[g, pl.ds(i * 128, 128), :]
-
-    def reduce_step(j):
-        v = share(j - 8)
+        return part[g, pl.ds(i * 128 + p * (128 // RP), 128 // RP), :]
+
+    def reduce_step(j, p):
+        cut = pl.ds(p * (128 // RP), 128 // RP)
+        v = share(j - 8, p)
         if j > 0:
-            landed(drecv.at[j - 1], d_r.at[j - 1])
-            v = v + drecv[j - 1].astype(F32)
-        dsend[j] = v.astype(BF)
-        remote(dsend.at[j], drecv.at[j], d_s.at[j], d_r.at[j], z_dn)
+            landed(drecv.at[j - 1, cut, :], d_r.at[j - 1, p])
+            v = v + drecv[j - 1, cut, :].astype(F32)
+        dsend[j, cut, :] = v.astype(BF)
+        remote(dsend.at[j, cut, :], drecv.at[j, cut, :], d_s.at[j, p], d_r.at[j, p], z_dn)
         if j > 0:
-            landed(urecv.at[j - 1], u_r.at[j - 1])
+            landed(urecv.at[j - 1, cut, :], u_r.at[j - 1, p])
         if j < 7:
-            v = share(7 - j)
+            v = share(7 - j, p)
             if j > 0:
-                v = v + urecv[j - 1].astype(F32)
-            usend[j] = v.astype(BF)
-            remote(usend.at[j], urecv.at[j], u_s.at[j], u_r.at[j], z_up)
+                v = v + urecv[j - 1, cut, :].astype(F32)
+            usend[j, cut, :] = v.astype(BF)
+            remote(usend.at[j, cut, :], urecv.at[j, cut, :], u_s.at[j, p], u_r.at[j, p], z_up)
+
+    def finish(p):
+        cut = pl.ds(p * (128 // RP), 128 // RP)
+        landed(drecv.at[7, cut, :], d_r.at[7, p])
+        out_ref[cut, :] = (
+            share(0, p) + urecv[6, cut, :].astype(F32) + drecv[7, cut, :].astype(F32)
+        ).astype(BF)
 
     steps = {
         "A": gather_step, "S": select, "Y": rows_out, "X": rows_forward, "Z": rows_last, "M": first_matmul,
         "H": hidden_out, "I": hidden_forward, "J": hidden_last, "N": second_matmul, "C": combine, "R": reduce_step,
     }
     for name in ORDER:
-        steps[name[0]](int(name[1:]))
-
-    landed(drecv.at[7], d_r.at[7])
-    out_ref[...] = (share(0) + urecv[6].astype(F32) + drecv[7].astype(F32)).astype(BF)
+        steps[name[0]](*map(int, name[1:].split(".")))
+    for p in range(RP):
+        finish(p)
     for c in pend:
         c.wait_send()
 
@@ -339,12 +355,12 @@
             pltpu.VMEM((8, 128, feat), BF),
             pltpu.VMEM((7, 128, feat), BF),
             dma, dma,
-            dma((16,)), dma((16,)), dma((16,)), dma((16,)),
+            dma((16, AP)), dma((16, AP)), dma((16,)), dma((16,)),
             dma((4, 4)), dma((4, 4)),
             dma((4, 4)), dma((4, 4)), dma((4, 4)), dma((4, 4)),
             dma((4,)), dma((4,)), dma((4, 4)), dma((4, 4)), dma((4, 4)), dma((4, 4)),
             dma((4, 4)), dma((4, 4)),
-            dma((8,)), dma((8,)), dma((7,)), dma((7,)),
+            dma((8, RP)), dma((8, RP)), dma((7, RP)), dma((7, RP)),
         ],
         compiler_params=pltpu.CompilerParams(
             collective_id=0, has_side_effects=True, vmem_limit_bytes=56 * 1024 * 1024

time: 166 us -> 134 us (0.81)
  the two profiles are of different devices: /device:TPU:66 before, /device:TPU:24 now
where the time goes in v2:
time: 134 us; the launch traced here: 132 us
  Pallas kernels  129 us (96%)
  local copies, waits for them, and re-layouts  1.57 us (1%)
    pallas_call x1, Pallas kernels, shards(): pl.pallas_call(kernel, out_shape=jax.ShapeDtypeStruct(tokens.shape, BF),...  129 us

profile of v2, /device:TPU:24, one launch (start us, length us, event | category | flops | bytes accessed | tf_op | source)
XLA Modules:
  0.0 132.2 jit_solution(10327014068494448402)
XLA Ops:
  0.0 0.7 convert_bitcast_fusion
  0.7 0.6 pad_maximum_fusion.route_in
  1.3 129.3 %shard_map.55 = bf16[128,512]{1,0:T(8,128)(2,1)} custom-call(bf16[128,512]{1,0:T(8,128)(2,1)} %tok_in.1, bf16[16,128]{1,0:T(8,128)(2,1)} %pad_maximum_fusion.route_in, bf16[1,4096,384]{2,1,0:T(8,128)(2,1)} %wgu_hbm.1, bf16[1,1536,512]{2,1,0:T(8,128)(2,1)} %wd_hbm.1), custom_call_target="tpu_custom_call" | custom-call | tf_op jit(solution)/shard_map/pallas_call | solution.py:327
  130.6 1.6 %copy.7 = bf16[128,512]{1,0:T(8,128)(2,1)} copy(bf16[128,512]{1,0:T(8,128)(2,1)} %shard_map.55) | data formatting | bytes 262144

commit v3 on v2

--- a/solution.py
+++ b/solution.py
@@ -13,23 +13,28 @@
 
 NX, NY, NZ = 4, 4, 16
 CAP = 20
+DIRECT = ()
 AP, RP = 2, 4
 GROUPS = ((6, -7, 7, -8), (4, -5, 5, -6), (2, -3, 3, -4), (0, -1, 1, -2))
 PLACE = {off: (g, i) for g, offs in enumerate(GROUPS) for i, off in enumerate(offs)}
 ORDER = (
-    "A1.0", "A1.1", "A2.0", "A2.1", "S3", "A3.0", "A3.1", "A4.0", "Y3", "A4.1", "S2", "A5.1",
-    "Y2", "A5.0", "A6.1", "A7.1", "X3", "A6.0", "S1", "X2", "A8.1", "A7.0", "Y1", "Z3",
-    "A8.0", "S0", "Z2", "M2", "Y0", "M3", "X0", "X1", "H2", "Z0", "M0", "H0",
-    "H3", "Z1", "M1", "I0", "H1", "J0", "I3", "N0", "I1", "I2", "J3", "C0",
-    "R0.1", "R0.3", "J1", "R0.2", "R0.0", "J2", "N1", "R1.1", "R1.2", "R1.0", "R1.3", "N2",
-    "C1", "R2.1", "R2.0", "R2.3", "R2.2", "N3", "R3.1", "R3.0", "C2", "R3.3", "R3.2", "R4.1",
-    "R4.0", "R4.3", "R4.2", "C3", "R5.1", "R5.0", "R5.3", "R5.2", "R6.1", "R6.0", "R6.3", "R6.2",
-    "R7.1", "R7.0", "R7.3", "R7.2",
+    "A1.0", "A1.1", "A2.0", "A2.1", "S3", "Y3.0", "A3.0", "A3.1", "X3.0", "A4.0", "Y3.1", "Y3.2",
+    "A4.1", "Y3.3", "S2", "A5.0", "X3.1", "Y2.0", "A5.1", "X3.2", "A6.0", "Y2.1", "A6.1", "S1",
+    "Y1.0", "X2.0", "A7.0", "Z3.2", "A7.1", "X3.3", "Y1.2", "X2.1", "Y1.3", "A8.0", "A8.1", "S0",
+    "Y0.0", "X1.0", "X1.2", "Y0.2", "Z3.3", "Z2.0", "Z2.1", "Y0.3", "Y0.1", "X0.0", "M3.1", "X0.2",
+    "X0.3", "Y1.1", "X1.3", "M2.0", "X0.1", "Y2.2", "Y2.3", "Z0.2", "Z0.0", "Z0.3", "Z3.1", "M0.1",
+    "Z0.1", "H0.1", "X1.1", "M0.0", "Z1.2", "X2.2", "Z1.3", "H0.0", "M1.1", "Z1.0", "I0.1", "Z1.1",
+    "H1.1", "M1.0", "X2.3", "I0.0", "H1.0", "Z2.2", "H3.1", "J0.1", "I1.1", "N0.1", "H2.0", "J0.0",
+    "Z2.3", "Z3.0", "N0.0", "I1.0", "M2.1", "J1.1", "H2.1", "N1.1", "J1.0", "C0", "R0.1", "R0.2",
+    "N1.0", "R0.3", "R0.0", "I2.1", "M3.0", "R1.1", "I2.0", "I3.1", "R1.2", "H3.0", "R1.3", "J2.1",
+    "R1.0", "C1", "N2.1", "R2.1", "J2.0", "R2.2", "J3.1", "R2.3", "N2.0", "R2.0", "I3.0", "R3.1",
+    "R3.2", "R3.3", "N3.1", "R3.0", "C2", "R4.1", "J3.0", "R4.2", "R4.3", "N3.0", "R4.0", "R5.1",
+    "R5.2", "R5.3", "R5.0", "C3", "R6.1", "R6.2", "R6.3", "R6.0", "R7.1", "R7.2", "R7.3", "R7.0",
 )
 
 
 def kernel(
-    tok_in, route_in, wgu_hbm, wd_hbm, out_ref,
+    tok_in, ids_in, nums_in, wgu_hbm, wd_hbm, out_ref,
     tok, route, wgu, wd, wsel, ysend, xfull, acc1, hx_send, hx_recv, hfull, acc2, ret, back, part,
     dsend, usend, drecv, urecv,
     wg_sem, wd_sem, tok_s, tok_r, rt_s, rt_r, y_s, y_r, x_s, x_r, xc_s, xc_r,
@@ -44,7 +49,8 @@
     x_up = (((x + 1) % NX) * 2 + core, exp)
     x_dn = (((x + NX - 1) % NX) * 2 + core, exp)
     sib = (x * 2 + (1 - core), exp)
-    peers = [z_up, z_dn, y_at[1], y_at[2], y_at[3], x_up, x_dn, sib]
+    x_far = (((x + 2) % NX) * 2 + core, exp)
+    peers = [z_up, z_dn, y_at[1], y_at[2], y_at[3], x_up, x_dn, sib] + ([x_far] if DIRECT else [])
 
     rows = NY * 4 * CAP
     quarter = 4 * CAP
@@ -100,12 +106,12 @@
             remote(rsrc, rd, rt_s.at[k], rt_r.at[k], dev)
         remote(src.at[cut, :], td.at[cut, :], tok_s.at[k, p], tok_r.at[k, p], dev)
 
+    own_t, own_r = tslot(0)
+    own_r[...] = jnp.concatenate([ids_in[...], nums_in[...]], axis=0).astype(F32).astype(BF)
     for p in range(AP):
-        send_block(tok_in, route_in, -1, z_up, p)
-        send_block(tok_in, route_in, 1, z_dn, p)
-    own_t, own_r = tslot(0)
+        send_block(tok_in, own_r, -1, z_up, p)
+        send_block(tok_in, own_r, 1, z_dn, p)
     own_t[...] = tok_in[...]
-    own_r[...] = route_in[...]
 
     tri = (
         lax.broadcasted_iota(jnp.int32, (128, 128), 0) < lax.broadcasted_iota(jnp.int32, (128, 128), 1)
@@ -149,7 +155,7 @@
             sel_cols.append(jnp.concatenate(col, axis=0).astype(BF))
         sel = jnp.concatenate(sel_cols, axis=1)
         picked = jnp.dot(sel, tok[g], preferred_element_type=F32).astype(BF)
-        for o in range(1, NY):
+        for o in (2, 1, 3):
             ysend[g, pl.ds(o * quarter, quarter), :] = picked[o * quarter:(o + 1) * quarter]
             to = (NY - o) % NY
             remote(
@@ -159,45 +165,53 @@
             )
         xfull[g, 0, pl.ds(0, quarter), :] = picked[:quarter]
 
-    def rows_out(g):
-        for o in range(1, NY):
-            landed(xfull.at[g, 0, pl.ds(o * quarter, quarter), :], y_r.at[g, o])
-        own = xfull.at[g, 0]
-        remote(own, xfull.at[g, 6], x_s.at[g, 0], x_r.at[g, 0], x_up)
-        remote(own, xfull.at[g, 2], x_s.at[g, 1], x_r.at[g, 1], x_dn)
-        remote(own, xfull.at[g, 1], xc_s.at[g, 0], xc_r.at[g, 0], sib)
-
-    def rows_forward(g):
-        lo, hi = pl.ds(0, half), pl.ds(half, half)
-        landed(xfull.at[g, 6], x_r.at[g, 0])
-        remote(xfull.at[g, 6, lo, :], xfull.at[g, 4, lo, :], x_s.at[g, 2], x_r.at[g, 2], x_up)
-        remote(xfull.at[g, 6], xfull.at[g, 7], xc_s.at[g, 1], xc_r.at[g, 1], sib)
-        landed(xfull.at[g, 2], x_r.at[g, 1])
-        remote(xfull.at[g, 2, hi, :], xfull.at[g, 4, hi, :], x_s.at[g, 3], x_r.at[g, 3], x_dn)
-        remote(xfull.at[g, 2], xfull.at[g, 3], xc_s.at[g, 2], xc_r.at[g, 2], sib)
-
-    def rows_last(g):
-        lo, hi = pl.ds(0, half), pl.ds(half, half)
-        landed(xfull.at[g, 4, lo, :], x_r.at[g, 2])
-        landed(xfull.at[g, 4, hi, :], x_r.at[g, 3])
-        remote(xfull.at[g, 4], xfull.at[g, 5], xc_s.at[g, 3], xc_r.at[g, 3], sib)
+    def piece(q):
+        return pl.ds(q * quarter, quarter)
+
+    def rows_out(g, q):
+        if q:
+            landed(xfull.at[g, 0, piece(q), :], y_r.at[g, q])
+        own = xfull.at[g, 0, piece(q), :]
+        remote(own, xfull.at[g, 6, piece(q), :], x_s.at[g, 0, q], x_r.at[g, 0, q], x_up)
+        remote(own, xfull.at[g, 2, piece(q), :], x_s.at[g, 1, q], x_r.at[g, 1, q], x_dn)
+        remote(own, xfull.at[g, 1, piece(q), :], xc_s.at[g, 0, q], xc_r.at[g, 0, q], sib)
+
+    def rows_forward(g, q):
+        low, high = xfull.at[g, 6, piece(q), :], xfull.at[g, 2, piece(q), :]
+        landed(low, x_r.at[g, 0, q])
+        landed(high, x_r.at[g, 1, q])
+        far = xfull.at[g, 4, piece(q), :]
+        if q < 2:
+            remote(low, far, x_s.at[g, 2, q], x_r.at[g, 2, q], x_up)
+        else:
+            remote(high, far, x_s.at[g, 2, q], x_r.at[g, 2, q], x_dn)
+        remote(low, xfull.at[g, 7, piece(q), :], xc_s.at[g, 1, q], xc_r.at[g, 1, q], sib)
+        remote(high, xfull.at[g, 3, piece(q), :], xc_s.at[g, 2, q], xc_r.at[g, 2, q], sib)
+
+    def rows_last(g, q):
+        landed(xfull.at[g, 4, piece(q), :], x_r.at[g, 2, q])
+        remote(
+            xfull.at[g, 4, piece(q), :], xfull.at[g, 5, piece(q), :], xc_s.at[g, 3, q], xc_r.at[g, 3, q], sib
+        )
 
     state = {"w1": False, "w2": False}
 
-    def first_matmul(g):
+    def first_matmul(g, h):
         if not state["w1"]:
             pltpu.make_async_copy(wgu, wgu, wg_sem).wait()
             state["w1"] = True
-        for i, s in enumerate((1, 7, 3, 5)):
-            landed(xfull.at[g, s], xc_r.at[g, i])
-        acc1[...] = jnp.dot(xfull[g, 0], wgu[0], preferred_element_type=F32)
+        for q in (2 * h, 2 * h + 1):
+            for i, s in enumerate((1, 7, 3, 5)):
+                landed(xfull.at[g, s, piece(q), :], xc_r.at[g, i, q])
+        span = pl.ds(h * half, half)
+        acc1[...] = jnp.dot(xfull[g, 0, span, :], wgu[0], preferred_element_type=F32)
 
         def body(s, carry):
-            acc1[...] += jnp.dot(xfull[g, s], wgu[s], preferred_element_type=F32)
+            acc1[...] += jnp.dot(xfull[g, s, span, :], wgu[s], preferred_element_type=F32)
             return carry
 
         lax.fori_loop(1, nsec, body, 0)
-        lane = lax.broadcasted_iota(jnp.int32, (rows, 128), 1)
+        lane = lax.broadcasted_iota(jnp.int32, (half, 128), 1)
         parts = []
         for b in range(3):
             v = acc1[:, b * 128:(b + 1) * 128]
@@ -206,69 +220,73 @@
             gate = jnp.where(low, v, other)
             up = jnp.where(low, other, v)
             parts.append(gate / (1.0 + jnp.exp(-gate)) * up)
-        hx_send[g, :, 0:128] = jnp.where(lane < 64, parts[0], parts[1]).astype(BF)
-        hx_send[g, :, 128:256] = parts[2].astype(BF)
-        remote(
-            hx_send.at[g, pl.ds(pl.multiple_of((1 - core) * half, half), half), :],
-            hx_recv.at[g], hx_s.at[g], hx_r.at[g], sib,
-        )
-
-    mine = pl.ds(pl.multiple_of(core * half, half), half)
-    mine_lo = pl.ds(pl.multiple_of(core * half, half // 2), half // 2)
-    mine_hi = pl.ds(pl.multiple_of(core * half + half // 2, half // 2), half // 2)
-    theirs = pl.ds(pl.multiple_of((1 - core) * half, half), half)
-
-    def hidden_out(g):
-        landed(hx_recv.at[g], hx_r.at[g])
+        hx_send[g, span, 0:128] = jnp.where(lane < 64, parts[0], parts[1]).astype(BF)
+        hx_send[g, span, 128:256] = parts[2].astype(BF)
+        remote(hx_send.at[g, owned(h, 1 - core), :], hx_recv.at[g, h], hx_s.at[g, h], hx_r.at[g, h], sib)
+
+    def owned(h, c):
+        return pl.ds(pl.multiple_of(h * half + c * quarter, quarter), quarter)
+
+    def hidden_out(g, h):
+        landed(hx_recv.at[g, h], hx_r.at[g, h])
+        mine = owned(h, core)
         a = hx_send[g, mine, :].astype(F32)
-        b = hx_recv[g].astype(F32)
+        b = hx_recv[g, h].astype(F32)
         zero = core == 0
         first = jnp.where(zero, a, b)
         second = jnp.where(zero, b, a)
-        lane = lax.broadcasted_iota(jnp.int32, (half, 128), 1)
+        lane = lax.broadcasted_iota(jnp.int32, (quarter, 128), 1)
         hfull[g, 0, mine, 0:128] = first[:, :128].astype(BF)
         hfull[g, 0, mine, 128:256] = jnp.where(lane < 64, first[:, 128:], second[:, 128:]).astype(BF)
         hfull[g, 0, mine, 256:384] = second[:, :128].astype(BF)
         own = hfull.at[g, 0, mine, :]
-        remote(own, hfull.at[g, 3, mine, :], h_s.at[g, 0], h_r.at[g, 0], x_up)
-        remote(own, hfull.at[g, 1, mine, :], h_s.at[g, 1], h_r.at[g, 1], x_dn)
-        remote(own, hfull.at[g, 0, mine, :], hc_s.at[g, 0], hc_r.at[g, 0], sib)
-
-    def hidden_forward(g):
-        landed(hfull.at[g, 3, mine, :], h_r.at[g, 0])
-        remote(hfull.at[g, 3, mine_lo, :], hfull.at[g, 2, mine_lo, :], h_s.at[g, 2], h_r.at[g, 2], x_up)
-        remote(hfull.at[g, 3, mine, :], hfull.at[g, 3, mine, :], hc_s.at[g, 3], hc_r.at[g, 3], sib)
-        landed(hfull.at[g, 1, mine, :], h_r.at[g, 1])
-        remote(hfull.at[g, 1, mine_hi, :], hfull.at[g, 2, mine_hi, :], h_s.at[g, 3], h_r.at[g, 3], x_dn)
-        remote(hfull.at[g, 1, mine, :], hfull.at[g, 1, mine, :], hc_s.at[g, 1], hc_r.at[g, 1], sib)
-
-    def hidden_last(g):
-        landed(hfull.at[g, 2, mine_lo, :], h_r.at[g, 2])
-        landed(hfull.at[g, 2, mine_hi, :], h_r.at[g, 3])
-        remote(hfull.at[g, 2, mine, :], hfull.at[g, 2, mine, :], hc_s.at[g, 2], hc_r.at[g, 2], sib)
-
-    def second_matmul(g):
+        if g in DIRECT:
+            remote(own, hfull.at[g, 2, mine, :], h_s.at[g, 2, h], h_r.at[g, 2, h], x_far)
+        remote(own, hfull.at[g, 3, mine, :], h_s.at[g, 0, h], h_r.at[g, 0, h], x_up)
+        remote(own, hfull.at[g, 1, mine, :], h_s.at[g, 1, h], h_r.at[g, 1, h], x_dn)
+        remote(own, hfull.at[g, 0, mine, :], hc_s.at[g, 0, h], hc_r.at[g, 0, h], sib)
+
+    def hidden_forward(g, h):
+        mine = owned(h, core)
+        low, high, far = hfull.at[g, 3, mine, :], hfull.at[g, 1, mine, :], hfull.at[g, 2, mine, :]
+        landed(low, h_r.at[g, 0, h])
+        landed(high, h_r.at[g, 1, h])
+        if g not in DIRECT:
+            if h == 0:
+                remote(low, far, h_s.at[g, 2, h], h_r.at[g, 2, h], x_up)
+            else:
+                remote(high, far, h_s.at[g, 2, h], h_r.at[g, 2, h], x_dn)
+        remote(low, low, hc_s.at[g, 3, h], hc_r.at[g, 3, h], sib)
+        remote(high, high, hc_s.at[g, 1, h], hc_r.at[g, 1, h], sib)
+
+    def hidden_last(g, h):
+        far = hfull.at[g, 2, owned(h, core), :]
+        landed(far, h_r.at[g, 2, h])
+        remote(far, far, hc_s.at[g, 2, h], hc_r.at[g, 2, h], sib)
+
+    def second_matmul(g, h):
         if not state["w2"]:
             pltpu.make_async_copy(wd, wd, wd_sem).wait()
             state["w2"] = True
+        theirs = owned(h, 1 - core)
         for o in range(NX):
-            landed(hfull.at[g, o, theirs, :], hc_r.at[g, o])
-        acc2[...] = jnp.dot(hfull[g, 0], wd[0], preferred_element_type=F32)
+            landed(hfull.at[g, o, theirs, :], hc_r.at[g, o, h])
+        span = pl.ds(h * half, half)
+        acc2[...] = jnp.dot(hfull[g, 0, span, :], wd[0], preferred_element_type=F32)
 
         def body(o, carry):
-            acc2[...] += jnp.dot(hfull[g, o], wd[o], preferred_element_type=F32)
+            acc2[...] += jnp.dot(hfull[g, o, span, :], wd[o], preferred_element_type=F32)
             return carry
 
         lax.fori_loop(1, NX, body, 0)
-        for o in range(1, NY):
-            ret[g, pl.ds(o * quarter, quarter), :] = acc2[pl.ds(o * quarter, quarter), :].astype(BF)
-            to = (NY - o) % NY
-            remote(
-                ret.at[g, pl.ds(o * quarter, quarter), :],
-                back.at[g, pl.ds(to * quarter, quarter), :],
-                b_s.at[g, to], b_r.at[g, to], y_at[o],
-            )
-        back[g, pl.ds(0, quarter), :] = acc2[pl.ds(0, quarter), :].astype(BF)
+        for o in (2 * h, 2 * h + 1):
+            done = acc2[pl.ds((o - 2 * h) * quarter, quarter), :].astype(BF)
+            if o == 0:
+                back[g, piece(0), :] = done
+                continue
+            ret[g, piece(o), :] = done
+            to = NY - o
+            remote(ret.at[g, piece(o), :], back.at[g, piece(to), :], b_s.at[g, to], b_r.at[g, to], y_at[o])
 
     def combine(g):
         for o in range(1, NY):
@@ -318,7 +336,6 @@
 
 
 def shards(tokens, expert_ids, numerators, gate_up_weight, down_weight):
-    route = jnp.concatenate([expert_ids.T, numerators.T], axis=0).astype(BF)
     feat = tokens.shape[1]
     rows = NY * 4 * CAP
     cols = gate_up_weight.shape[2]
@@ -328,6 +345,7 @@
         kernel,
         out_shape=jax.ShapeDtypeStruct(tokens.shape, BF),
         in_specs=[
+            pl.BlockSpec(memory_space=pltpu.VMEM),
             pl.BlockSpec(memory_space=pltpu.VMEM),
             pl.BlockSpec(memory_space=pltpu.VMEM),
             pl.BlockSpec(memory_space=pl.ANY),
@@ -342,11 +360,11 @@
             pltpu.VMEM((4, rows, 512), BF),
             pltpu.VMEM((4, rows, feat), BF),
             pltpu.VMEM((4, 8, rows, feat), BF),
-            pltpu.VMEM((rows, cols), F32),
+            pltpu.VMEM((rows // 2, cols), F32),
             pltpu.VMEM((4, rows, 256), BF),
-            pltpu.VMEM((4, rows // 2, 256), BF),
+            pltpu.VMEM((4, 2, rows // 4, 256), BF),
             pltpu.VMEM((4, NX, rows, units), BF),
-            pltpu.VMEM((rows, feat), F32),
+            pltpu.VMEM((rows // 2, feat), F32),
             pltpu.VMEM((4, rows, feat), BF),
             pltpu.VMEM((4, rows, feat), BF),
             pltpu.VMEM((4, 512, feat), F32),
@@ -357,15 +375,15 @@
             dma, dma,
             dma((16, AP)), dma((16, AP)), dma((16,)), dma((16,)),
             dma((4, 4)), dma((4, 4)),
-            dma((4, 4)), dma((4, 4)), dma((4, 4)), dma((4, 4)),
-            dma((4,)), dma((4,)), dma((4, 4)), dma((4, 4)), dma((4, 4)), dma((4, 4)),
+            dma((4, 3, 4)), dma((4, 3, 4)), dma((4, 4, 4)), dma((4, 4, 4)),
+            dma((4, 2)), dma((4, 2)), dma((4, 3, 2)), dma((4, 3, 2)), dma((4, 4, 2)), dma((4, 4, 2)),
             dma((4, 4)), dma((4, 4)),
             dma((8, RP)), dma((8, RP)), dma((7, RP)), dma((7, RP)),
         ],
         compiler_params=pltpu.CompilerParams(
             collective_id=0, has_side_effects=True, vmem_limit_bytes=56 * 1024 * 1024
         ),
-    )(tokens, route, gate_up_weight, down_weight)
+    )(tokens, expert_ids.T, numerators.T, gate_up_weight, down_weight)
 
 
 def solution(mesh):

time: 134 us -> 125 us (0.933)
  Pallas kernels: 129 us -> 123 us
    pallas_call x1, Pallas kernels: 129 us -> 123 us  [shards(): pl.pallas_call(kernel, out_shape=jax.ShapeDtypeStruct(tokens.shape, BF),...]
where the time goes in v3:
time: 125 us; the launch traced here: 124 us
  Pallas kernels  123 us (98%)
  local copies, waits for them, and re-layouts  1.57 us (1%)
    pallas_call x1, Pallas kernels, shards(): pl.pallas_call(kernel, out_shape=jax.ShapeDtypeStruct(tokens.shape, BF),...  123 us

profile of v3, /device:TPU:24, one launch (start us, length us, event | category | flops | bytes accessed | tf_op | source)
XLA Modules:
  0.0 124.4 jit_solution(16744528077300760244)
XLA Ops:
  0.0 122.8 %shard_map.55 = bf16[128,512]{1,0:T(8,128)(2,1)} custom-call(bf16[128,512]{1,0:T(8,128)(2,1)} %tok_in.1, s32[8,128]{1,0:T(8,128)} %bitcast.2, s32[8,128]{1,0:T(8,128)} %bitcast.3, bf16[1,4096,384]{2,1,0:T(8,128)(2,1)} %wgu_hbm.1, bf16[1,1536,512]{2,1,0:T(8,128)(2,1)} %wd_hbm.1), custom_call_target="tpu_custom_call" | custom-call | tf_op jit(solution)/shard_map/pallas_call | solution.py:344
  122.8 1.6 %copy.7 = bf16[128,512]{1,0:T(8,128)(2,1)} copy(bf16[128,512]{1,0:T(8,128)(2,1)} %shard_map.55) | data formatting | bytes 262144
